TPU v7x, 128 devices: a whole 4x4x4 slice. The times are simulated.
128 devices in a mesh: section: 4 (over z), scan: 32 (over x, y, core).
Axes of the slice: x: 4, y: 4, z: 4, core: 2. Of those that a mesh axis runs over, the one named last changes fastest.
Arguments:
- frames: bfloat16 [128, 1024, 2048], P('scan', None, 'section'), may hold values from -6 to 6
- increments: int32 [128], P('scan'), may hold values from 1 to 2
- resample: bfloat16 [256, 32, 32], replicated, may hold values from -1 to 2
- wigner_filter: bfloat16 [2, 128, 1024, 2048], P(None, None, ('section', 'scan')), may hold values from -6 to 6
Outputs:
- deconvolved: bfloat16 [2, 128, 1024, 2048], P(None, None, ('section', 'scan'))
Inputs may be any that keep to these rules, and one draw needn't show every extreme that they name: `increments`: each scan row advances the descan drift by one or two table entries.
All inputs are finite; a program needn't handle non-finite values.
Results may differ from a plain program's by a relative error of at most 0.0066.
Values may be sent and summed in bfloat16 or wider, within the bound.
A program may use at most 192 MiB of HBM per device.

v0:
```python
import math

import jax
import jax.numpy as jnp
from jax import lax
from jax.sharding import PartitionSpec as P


def entering(x, axis, combine, identity):
    devices, place = (lax.axis_size(axis), lax.axis_index(axis))
    everything = lax.all_gather(x, axis)
    start = jnp.broadcast_to(jnp.asarray(identity, x.dtype), x.shape)

    def hop(k, before):
        reached = k < place
        new = combine(before, everything[k])
        return jnp.where(reached, new, before)

    return lax.fori_loop(0, devices, hop, start)


def fast_matrix(length):
    steps_p = jnp.arange(length, dtype=jnp.int32)
    phase = steps_p[:, None] * steps_p[None, :] % length
    angle = phase.astype(jnp.float32) * (2.0 * math.pi / length)
    return jnp.concatenate([jnp.cos(angle), -jnp.sin(angle)], axis=0).astype(jnp.bfloat16)


def slow_matrix(row_order, length):
    frequency = jnp.arange(length, dtype=jnp.int32)
    phase = frequency[:, None] * row_order[None, :] % length
    angle = phase.astype(jnp.float32) * (2.0 * math.pi / length)
    cosine = jnp.cos(angle)
    sine = jnp.sin(angle)
    upper = jnp.stack([cosine, sine], axis=1)
    lower = jnp.stack([-sine, cosine], axis=1)
    return jnp.stack([upper, lower], axis=0).astype(jnp.bfloat16)


def add_counts(earlier, later):
    return earlier + later


def slow_apply(slow_table, arrived, slow_scale):
    return (
        jnp.einsum("aybr,bxrk->ayxk", slow_table, arrived, preferred_element_type=jnp.float32)
        * slow_scale
    )


def apply_descan(matrices, incoming, detector_rows):
    shape_in = incoming.shape
    blocked = incoming.reshape(shape_in[0], shape_in[1], shape_in[2], detector_rows, -1)
    shifted = jnp.einsum("rab,cqrbx->cqrax", matrices, blocked, preferred_element_type=jnp.float32)
    return shifted.reshape(shape_in[0], shape_in[1], shape_in[2], -1).astype(jnp.bfloat16)


def shards(frames, increments, resample, wigner_filter):
    section_count = lax.axis_size("section")
    scan_count = lax.axis_size("scan")
    group_rows = frames.shape[0]
    positions = frames.shape[1]
    rows_dev = group_rows // section_count
    total_rows = group_rows * scan_count
    detector_rows = resample.shape[1]
    section_at = lax.axis_index("section")
    fast_table = fast_matrix(positions).reshape(2, positions, positions)
    raw = jnp.einsum("cqp,rpk->cqrk", fast_table, frames, preferred_element_type=jnp.float32)
    raw = (raw * (1.0 / math.sqrt(positions))).astype(jnp.bfloat16)
    slow_scale = 1.0 / math.sqrt(total_rows)
    local_sum = jnp.cumsum(increments)
    block_total = local_sum[group_rows - 1]
    before = entering(block_total, "scan", add_counts, jnp.int32(0))
    shift_index = before + lax.dynamic_slice_in_dim(local_sum, section_at * rows_dev, rows_dev) - 1
    matrices = resample[shift_index]
    spectrum = apply_descan(
        matrices,
        lax.all_to_all(raw, "section", split_axis=2, concat_axis=3, tiled=True),
        detector_rows,
    )
    device_count = section_count * scan_count
    linear = jnp.arange(device_count, dtype=jnp.int32)
    first_row = linear % scan_count * group_rows + linear // scan_count * rows_dev
    row_order = (first_row[:, None] + jnp.arange(rows_dev, dtype=jnp.int32)[None, :]).reshape(-1)
    slow_table = slow_matrix(row_order, total_rows)
    slow_grid = slow_apply(
        slow_table,
        lax.all_to_all(spectrum, ("section", "scan"), split_axis=1, concat_axis=2, tiled=True),
        slow_scale,
    )
    filter_real = wigner_filter[0].astype(jnp.float32)
    filter_imag = wigner_filter[1].astype(jnp.float32)
    real_part = slow_grid[0] * filter_real - slow_grid[1] * filter_imag
    imag_part = slow_grid[0] * filter_imag + slow_grid[1] * filter_real
    return jnp.stack([real_part, imag_part]).astype(jnp.bfloat16)


def solution(mesh):
    in_specs = (
        P("scan", None, "section"),
        P("scan"),
        P(),
        P(None, None, ("section", "scan"), None),
    )
    out_specs = P(None, None, ("section", "scan"), None)
    return jax.shard_map(shards, mesh=mesh, in_specs=in_specs, out_specs=out_specs, check_vma=False)
```

profile of v0, /device:TPU:1, one launch (start us, length us, event | category | flops | bytes accessed | tf_op | source)
XLA Modules:
  0.0 365.1 jit_solution(17719723984195666189)
XLA Ops:
  0.0 17.0 %negate_convert_fusion = (bf16[1024,1024]{1,0:T(8,128)(2,1)S(1)}, bf16[1024,1024]{1,0:T(8,128)(2,1)S(1)}) fusion(), kind=kLoop, calls=%fused_computation.25 | loop fusion | flops 17825792 | bytes 4194304 | tf_op jit(solution)/shard_map/convert.3
  17.5 1.7 copy-done.2
  19.2 10.8 %multiply_convert_fusion = bf16[2,1024,4,512]{3,1,2,0:T(8,128)(2,1)} fusion(bf16[2,1024,1024,1]{2,1,3,0:T(8,128)(2,1)S(1)} %bitcast.56, bf16[4,1024,512]{2,1,0:T(8,128)(2,1)S(1)} %copy-done.2), kind=kOutput, calls=%fused_computation.1 | convolution fusion | flops 8598323200 | bytes 16777216 | tf_op jit(solution)/shard_map/cqp,rpk->cqrk/dot_general | solution.py:68
  30.1 7.2 %copy.17 = bf16[2,1024,4,512]{3,1,0,2:T(8,128)(2,1)} copy(bf16[2,1024,4,512]{3,1,2,0:T(8,128)(2,1)} %multiply_convert_fusion) | data formatting | bytes 16777216 | tf_op jit(solution)/shard_map/convert_element_type | solution.py:69
  37.2 6.0 %all-to-all-start = ((bf16[2,1024,4,512]{3,1,0,2:T(8,128)(2,1)}), bf16[2,1024,4,512]{3,1,0,2:T(8,128)(2,1)}, u32[]{:S(2)}, u32[]{:S(2)}) async-start(bf16[2,1024,4,512]{3,1,0,2:T(8,128)(2,1)} %copy.17), calls=%async_computation | async-start | bytes 16777216 | tf_op jit(solution)/shard_map/all_to_all | solution.py:78
  44.6 1.2 bitcast_dynamic-update-slice_fusion
  45.8 15.1 %all-reduce = s32[32]{0:T(128)S(1)} all-reduce(s32[32]{0:T(128)S(1)} %bitcast_dynamic-update-slice_fusion), channel_id=2, replica_groups=mesh['section'=4,'scan'=32] {'scan'}, use_global_device_ids=true, to_apply=%add | all-reduce | flops 32 | bytes 256 | tf_op jit(solution)/shard_map/all_gather | solution.py:11
  60.9 41.3 %while.14 = (s32[]{:T(128)}, s32[]{:T(128)}, s32[]{:T(128)}, s32[32]{0:T(128)S(1)}, s32[]{:T(128)}) while((s32[]{:T(128)}, s32[]{:T(128)}, s32[]{:T(128)}, s32[32]{0:T(128)S(1)}, s32[]{:T(128)}) %tuple.40), condition=%wide.region_2.3_spmd, body=%wide.region_1.2_spmd.sunk | while | flops 5 | bytes 115 | solution.py:19
  62.2 0.6 dynamic_slice.16
  63.5 0.6 dynamic_slice.16
  64.8 0.6 dynamic_slice.16
  66.1 0.6 dynamic_slice.16
  103.3 34.7 %all-to-all-done = bf16[2,1024,4,512]{3,1,0,2:T(8,128)(2,1)} async-done(((bf16[2,1024,4,512]{3,1,0,2:T(8,128)(2,1)}), bf16[2,1024,4,512]{3,1,0,2:T(8,128)(2,1)}, u32[]{:S(2)}, u32[]{:S(2)}) %all-to-all-start) | async-done | bytes 8388640 | tf_op jit(solution)/shard_map/all_to_all | solution.py:78
  138.0 11.7 %copy.18 = bf16[2,1024,4,512]{1,3,2,0:T(8,128)(2,1)} copy(bf16[2,1024,4,512]{3,1,0,2:T(8,128)(2,1)} %all-to-all-done) | data formatting | bytes 16777216 | tf_op jit(solution)/shard_map/all_to_all | solution.py:78
  149.7 18.4 %convert_bitcast_fusion = bf16[2,1024,1,32,64]{1,3,4,0,2:T(8,128)(2,1)} fusion(bf16[2,1024,32,64]{1,3,2,0:T(8,128)(2,1)} %bitcast.54, bf16[1,32,32]{2,1,0:T(8,128)(2,1)S(1)} %copy.34), kind=kOutput, calls=%fused_computation.16 | convolution fusion | flops 272629760 | bytes 16779264 | tf_op jit(solution)/shard_map/rab,cqrbx->cqrax/dot_general | solution.py:54
  168.1 22.0 %copy.21 = bf16[2,1024,1,32,64]{1,4,3,0,2:T(8,128)(2,1)} copy(bf16[2,1024,1,32,64]{1,3,4,0,2:T(8,128)(2,1)} %convert_bitcast_fusion) | data formatting | bytes 16777216 | tf_op jit(solution)/shard_map/convert_element_type | solution.py:55
  190.0 21.4 %copy.22 = bf16[2,1024,1,2048]{3,0,2,1:T(2,128)(2,1)} copy(bf16[2,1024,1,2048]{1,3,0,2:T(8,128)(2,1)} %bitcast.55) | data formatting | bytes 16777216 | tf_op jit(solution)/shard_map/convert_element_type | solution.py:55
  211.5 8.7 %all-to-all-start.1 = ((bf16[2,1024,1,2048]{3,0,2,1:T(2,128)(2,1)}), bf16[2,1024,1,2048]{3,0,2,1:T(2,128)(2,1)}, u32[]{:S(2)}, u32[]{:S(2)}) async-start(bf16[2,1024,1,2048]{3,0,2,1:T(2,128)(2,1)} %copy.22), calls=%async_computation.1 | async-start | bytes 16777216 | tf_op jit(solution)/shard_map/all_to_all | solution.py:88
  220.5 6.2 %fusion.34 = (bf16[1,128,8,2048]{3,2,1,0:T(8,128)(2,1)}, bf16[1,128,8,2048]{3,2,1,0:T(8,128)(2,1)}) fusion(bf16[2,128,8,2048]{3,2,1,0:T(8,128)(2,1)} %param.9), kind=kLoop, calls=%fused_computation.60 | loop fusion | bytes 16777216 | tf_op jit(solution)/shard_map/slice | solution.py:91
  226.6 91.5 %all-to-all-done.1 = bf16[2,1024,1,2048]{3,0,2,1:T(2,128)(2,1)} async-done(((bf16[2,1024,1,2048]{3,0,2,1:T(2,128)(2,1)}), bf16[2,1024,1,2048]{3,0,2,1:T(2,128)(2,1)}, u32[]{:S(2)}, u32[]{:S(2)}) %all-to-all-start.1) | async-done | bytes 8388640 | tf_op jit(solution)/shard_map/all_to_all | solution.py:88
  318.1 16.0 %bitcast_multiply_fusion = f32[2,128,8,2048]{3,1,2,0:T(8,128)S(1)} fusion(bf16[2,128,8,1,2048]{4,0,2,1,3:T(2,128)(2,1)} %bitcast.22, bf16[1,128,2,128]{3,1,2,0:T(8,128)(2,1)S(1)} %get-tuple-element.109, bf16[1,128,2,128]{3,1,2,0:T(8,128)(2,1)S(1)} %get-tuple-element.108), kind=kOutput, calls=%fused_computation | convolution fusion | flops 2151940096 | bytes 25296896 | tf_op jit(solution)/shard_map/aybr,bxrk->ayxk/dot_general | solution.py:46
  334.1 11.9 %fusion.1 = (bf16[1,128,8,2048]{3,1,2,0:T(8,128)(2,1)}, bf16[1,128,8,2048]{3,1,2,0:T(8,128)(2,1)}) fusion(f32[2,128,8,2048]{3,1,2,0:T(8,128)S(1)} %bitcast_multiply_fusion, bf16[1,128,8,2048]{3,2,1,0:T(8,128)(2,1)} %get-tuple-element.107, bf16[1,128,8,2048]{3,2,1,0:T(8,128)(2,1)} %get-tuple-element.106), kind=kLoop, calls=%fused_computation.7 | loop fusion | flops 20971520 | bytes 33554432 | tf_op jit(solution)/shard_map/convert
  346.0 7.5 %pad_maximum_fusion = bf16[2,128,8,2048]{3,1,2,0:T(8,128)(2,1)} fusion(bf16[1,128,8,2048]{3,1,2,0:T(8,128)(2,1)} %get-tuple-element.105, bf16[1,128,8,2048]{3,1,2,0:T(8,128)(2,1)} %get-tuple-element.104), kind=kLoop, calls=%fused_computation.10 | loop fusion | flops 4194304 | bytes 16777216 | tf_op jit(solution)/shard_map/stack | solution.py:95
  353.4 11.5 %copy.27 = bf16[2,128,8,2048]{3,2,1,0:T(8,128)(2,1)} copy(bf16[2,128,8,2048]{3,1,2,0:T(8,128)(2,1)} %pad_maximum_fusion) | data formatting | bytes 16777216 | tf_op jit(solution)/shard_map/stack | solution.py:95
  (47 shorter events, 20.5 us)
Async XLA Ops:
  0.0 102.9 %copy-start = (bf16[256,32,32]{0,2,1:T(8,128)(2,1)S(1)}, bf16[256,32,32]{0,2,1:T(8,128)(2,1)}, u32[]{:S(2)}) copy-start(bf16[256,32,32]{0,2,1:T(8,128)(2,1)} %param.8) | copy-start | bytes 1572868
  17.0 2.2 copy-start.2
  37.2 6.0 %copy-start.3 = (s32[4]{0:T(128)S(1)}, s32[4]{0:T(128)}, u32[]{:S(2)}) copy-start(s32[4]{0:T(128)} %param.7) | copy-start | bytes 52
  37.2 6.2 %copy-start.4 = (u32[128]{0:T(128)S(1)}, u32[128]{0:T(128)}, u32[]{:S(2)}) copy-start(u32[128]{0:T(128)} %constant.137) | copy-start | bytes 1540
  37.2 100.8 %all-to-all-start = ((bf16[2,1024,4,512]{3,1,0,2:T(8,128)(2,1)}), bf16[2,1024,4,512]{3,1,0,2:T(8,128)(2,1)}, u32[]{:S(2)}, u32[]{:S(2)}) async-start(bf16[2,1024,4,512]{3,1,0,2:T(8,128)(2,1)} %copy.17), calls=%async_computation | async-start | bytes 16777216 | tf_op jit(solution)/shard_map/all_to_all | solution.py:78
  211.5 106.7 %all-to-all-start.1 = ((bf16[2,1024,1,2048]{3,0,2,1:T(2,128)(2,1)}), bf16[2,1024,1,2048]{3,0,2,1:T(2,128)(2,1)}, u32[]{:S(2)}, u32[]{:S(2)}) async-start(bf16[2,1024,1,2048]{3,0,2,1:T(2,128)(2,1)} %copy.22), calls=%async_computation.1 | async-start | bytes 16777216 | tf_op jit(solution)/shard_map/all_to_all | solution.py:88
  353.4 11.5 %copy-start.1 = (bf16[256,32,32]{0,2,1:T(8,128)(2,1)S(1)}, bf16[256,32,32]{0,2,1:T(8,128)(2,1)}, u32[]{:S(2)}) copy-start(bf16[256,32,32]{0,2,1:T(8,128)(2,1)} %param.8) | copy-start | bytes 1572868
where the time goes:
time: 372 us; the launch traced here: 365 us
  waiting for transfers between devices  126 us (34%)
  local copies, waits for them, and re-layouts  105 us (28%)
  matrix products  45.2 us (12%)
  other arithmetic  37.3 us (10%)
  loops' own time  20.8 us (6%)
  blocking collectives  15.1 us (4%)
  starting transfers between devices  14.7 us (4%)
    all_to_all x1, waiting for transfers between devices, shards(): lax.all_to_all(spectrum, ('section', 'scan'), split_axis=1, concat_axis=2...  91.5 us
    convert_element_type x2, local copies, waits for them, and re-layouts, apply_descan(): shifted.reshape(shape_in[0], shape_in[1], shape_in[2], -1)  43.4 us
    all_to_all x1, waiting for transfers between devices, shards(): lax.all_to_all(raw, 'section', split_axis=2, concat_axis=3, tiled=True)  34.7 us
    another operation x4, other arithmetic  29.4 us
    another operation x1, loops' own time, entering(): return lax.fori_loop(0, devices, hop, start)  20.8 us
    dynamic_slice x32, local copies, waits for them, and re-layouts, hop(): new = combine(before, everything[k])  20.5 us
    dot_general x1, matrix products, apply_descan(): jnp.einsum('rab,cqrbx->cqrax', matrices, blocked, preferred_element_type=...  18.4 us
    dot_general x1, matrix products, slow_apply(): jnp.einsum('aybr,bxrk->ayxk', slow_table, arrived, preferred_element_type...  16 us
  transfers between devices with their start and end apart: 2, of which 2 were waited for; matrix products, arithmetic and copies ran while one was open for 8% of the time, Pallas kernels for 0%

commit v1 on v0

v1 whole, which is shorter than its diff:
```python
import math

import jax
import jax.numpy as jnp
from jax import lax
from jax.sharding import PartitionSpec as P


def fast_matrix(length):
    steps_p = jnp.arange(length, dtype=jnp.int32)
    phase = steps_p[:, None] * steps_p[None, :] % length
    angle = phase.astype(jnp.float32) * (2.0 * math.pi / length)
    return jnp.stack([jnp.cos(angle), -jnp.sin(angle)], axis=0).astype(jnp.bfloat16)


def slow_matrix(row_order, length):
    frequency = jnp.arange(length, dtype=jnp.int32)
    phase = frequency[:, None] * row_order[None, :] % length
    angle = phase.astype(jnp.float32) * (2.0 * math.pi / length)
    cosine = jnp.cos(angle)
    sine = jnp.sin(angle)
    upper = jnp.stack([cosine, sine], axis=1)
    lower = jnp.stack([-sine, cosine], axis=1)
    return jnp.stack([upper, lower], axis=0).astype(jnp.bfloat16)


def shards(frames, increments, resample, wigner_filter):
    section_count = lax.axis_size("section")
    scan_count = lax.axis_size("scan")
    devices = section_count * scan_count
    rows_loc, positions, pixels_loc = frames.shape
    total_rows = rows_loc * scan_count
    detector_rows = resample.shape[1]
    rows_sec = detector_rows // section_count
    detector_cols = pixels_loc // rows_sec
    q_loc = positions // devices

    fast_table = fast_matrix(positions).reshape(2, devices, q_loc, positions)
    raw = jnp.einsum("cdqp,rpk->dcqrk", fast_table, frames, preferred_element_type=jnp.float32)
    raw = (raw * (1.0 / math.sqrt(positions))).astype(jnp.bfloat16)
    got = lax.all_to_all(raw, ("section", "scan"), 0, 0, tiled=True)
    got = got.reshape(section_count, scan_count, 2, q_loc, rows_loc, rows_sec, detector_cols)

    every_increment = lax.all_gather(increments, "scan", tiled=True)
    shift_index = jnp.cumsum(every_increment) - 1
    matrices = resample[shift_index].reshape(scan_count, rows_loc, detector_rows, section_count, rows_sec)
    spectrum = jnp.einsum("jiasb,sjcqibx->cqjiax", matrices, got, preferred_element_type=jnp.float32)
    spectrum = spectrum.astype(jnp.bfloat16).reshape(2, q_loc, total_rows, detector_rows * detector_cols)

    slow_table = slow_matrix(jnp.arange(total_rows, dtype=jnp.int32), total_rows)
    slow_grid = jnp.einsum("aybr,bqrk->ayqk", slow_table, spectrum, preferred_element_type=jnp.float32)
    slow_grid = slow_grid * (1.0 / math.sqrt(total_rows))
    filter_real = wigner_filter[0].astype(jnp.float32)
    filter_imag = wigner_filter[1].astype(jnp.float32)
    real_part = slow_grid[0] * filter_real - slow_grid[1] * filter_imag
    imag_part = slow_grid[0] * filter_imag + slow_grid[1] * filter_real
    return jnp.stack([real_part, imag_part]).astype(jnp.bfloat16)


def solution(mesh):
    in_specs = (
        P("scan", None, "section"),
        P("scan"),
        P(),
        P(None, None, ("section", "scan"), None),
    )
    out_specs = P(None, None, ("section", "scan"), None)
    return jax.shard_map(shards, mesh=mesh, in_specs=in_specs, out_specs=out_specs, check_vma=False)
```

time: 372 us -> 284 us (0.76)
  waiting for transfers between devices: 126 us -> 0.01 us
  blocking collectives: 15.1 us -> 99.4 us
  loops' own time: 20.8 us -> 0 us
  matrix products: 45.2 us -> 33.8 us
  local copies, waits for them, and re-layouts: 105 us -> 95.3 us
    all_to_all x2 -> x1, waiting for transfers between devices: 126 us -> 0.01 us  [shards(): got = lax.all_to_all(raw, ('section', 'scan'), 0, 0, tiled=True)]
    unnamed x0 -> x1, blocking collectives: none -> 99.4 us
    reshape x0 -> x3, local copies, waits for them, and re-layouts: none -> 45.6 us  [the longest x1 23.4 us: shards(): spectrum.astype(jnp.bfloat16)]
    convert_element_type x2 -> x0, local copies, waits for them, and re-layouts: 43.4 us -> none  [apply_descan(): shifted.reshape(shape_in[0], shape_in[1], shape_in[2], -1)]
    dynamic_slice x33 -> x0, local copies, waits for them, and re-layouts: 21.1 us -> none  [the longest x32 20.5 us: hop(): new = combine(before, everything[k])]
    another operation x1 -> x0, loops' own time: 20.8 us -> none  [entering(): return lax.fori_loop(0, devices, hop, start)]
    all_gather x1 -> x0, blocking collectives: 15.1 us -> none  [entering(): everything = lax.all_gather(x, axis)]
    all_to_all x1 -> x0, local copies, waits for them, and re-layouts: 11.7 us -> none  [shards(): lax.all_to_all(raw, 'section', split_axis=2, concat_axis=3, tiled=True)]
  transfers between devices with their start and end apart: 2 -> 1, of which waited for: 2 -> 0; matrix products, arithmetic and copies ran while one was open for 8% -> 4% of each run, Pallas kernels for 0% -> 0%
where the time goes in v1:
time: 284 us; the launch traced here: 280 us
  blocking collectives  99.4 us (35%)
  local copies, waits for them, and re-layouts  95.3 us (34%)
  other arithmetic  38.6 us (14%)
  matrix products  33.8 us (12%)
  starting transfers between devices  11.9 us (4%)
    unnamed x1, blocking collectives  99.4 us
    another operation x5, other arithmetic  31 us
    reshape x1, local copies, waits for them, and re-layouts, shards(): spectrum.astype(jnp.bfloat16)  23.4 us
    reshape x1, local copies, waits for them, and re-layouts, shards(): got.reshape(section_count, scan_count, 2, q_loc, rows_loc, rows_sec, dete...  22 us
    convert_element_type x1, local copies, waits for them, and re-layouts, shards(): raw = (raw * (1.0 / math.sqrt(positions))).astype(jnp.bfloat16)  18.4 us
    dot_general x1, matrix products, shards(): jnp.einsum('aybr,bqrk->ayqk', slow_table, spectrum, preferred_element_typ...  15.8 us
    all_to_all x1, starting transfers between devices, shards(): got = lax.all_to_all(raw, ('section', 'scan'), 0, 0, tiled=True)  11.9 us
    another operation x1, local copies, waits for them, and re-layouts, shards(): return jnp.stack([real_part, imag_part]).astype(jnp.bfloat16)  11.4 us
  transfers between devices with their start and end apart: 1, of which 0 were waited for; matrix products, arithmetic and copies ran while one was open for 4% of the time, Pallas kernels for 0%

profile of v1, /device:TPU:1, one launch (start us, length us, event | category | flops | bytes accessed | tf_op | source)
XLA Modules:
  0.0 279.9 jit_solution(9770856101874589907)
XLA Ops:
  0.0 18.2 %cosine_convert_fusion = (bf16[1,128,8,1024]{3,1,2,0:T(8,128)(2,1)S(1)}, bf16[1,128,8,1024]{3,1,2,0:T(8,128)(2,1)S(1)}) fusion(s32[128,8]{0,1:T(8,128)S(1)} %multiply_add_fusion), kind=kLoop, calls=%fused_computation.31 | loop fusion | flops 17825792 | bytes 4198400 | tf_op jit(solution)/shard_map/convert.2
  18.2 9.5 %fusion.7 = bf16[128,2,8,4,512]{4,0,3,2,1:T(8,128)(2,1)S(1)} fusion(bf16[1,128,8,1024]{3,1,2,0:T(8,128)(2,1)S(1)} %get-tuple-element.12, bf16[1,128,8,1024]{3,1,2,0:T(8,128)(2,1)S(1)} %get-tuple-element.11, bf16[4,1024,512]{2,1,0:T(8,128)(2,1)S(1)} %copy-done.1), kind=kOutput, calls=%fused_computation.15 | convolution fusion | flops 8606711808 | bytes 16777216 | tf_op jit(solution)/shard_map/cdqp,rpk->dcqrk/dot_general | solution.py:39
  27.6 18.4 %copy.28 = bf16[128,2,8,4,512]{4,3,2,1,0:T(4,128)(2,1)} copy(bf16[128,2,8,4,512]{4,0,3,2,1:T(8,128)(2,1)S(1)} %fusion.7) | data formatting | bytes 16777216 | tf_op jit(solution)/shard_map/convert_element_type | solution.py:40
  46.1 11.9 %all-to-all-start = ((bf16[128,2,8,4,512]{4,3,2,1,0:T(4,128)(2,1)}), bf16[128,2,8,4,512]{4,3,2,1,0:T(4,128)(2,1)}, u32[]{:S(2)}, u32[]{:S(2)}) async-start(bf16[128,2,8,4,512]{4,3,2,1,0:T(4,128)(2,1)} %copy.28), calls=%async_computation | async-start | bytes 16777216 | tf_op jit(solution)/shard_map/all_to_all | solution.py:41
  58.0 3.0 %copy.31 = bf16[256,32,32]{2,1,0:T(8,128)(2,1)S(1)} copy(bf16[256,32,32]{0,2,1:T(8,128)(2,1)S(1)} %copy-done) | data formatting | bytes 1048576 | tf_op args[2]
  61.1 0.6 dynamic-slice
  62.4 0.2 dynamic-update-slice
  62.6 99.4 %all-reduce = s32[128]{0:T(128)S(1)} all-reduce(s32[128]{0:T(128)S(1)} %dynamic-update-slice), channel_id=1, replica_groups=mesh['section'=4,'scan'=32] {'scan'}, use_global_device_ids=true, to_apply=%add | all-reduce | flops 128 | bytes 1024
  162.0 0.1 copy.30
  162.1 0.2 reduce-window.4
  162.3 0.1 fusion.28
  162.4 0.8 gather_fusion
  163.2 0.6 copy.32
  163.8 0.3 fusion.33
  164.1 0.3 negate_convert_fusion.1
  164.4 6.0 %fusion.36 = (bf16[1,128,8,2048]{3,2,1,0:T(8,128)(2,1)}, bf16[1,128,8,2048]{3,2,1,0:T(8,128)(2,1)}) fusion(bf16[2,128,8,2048]{3,2,1,0:T(8,128)(2,1)} %param.7), kind=kLoop, calls=%fused_computation.60 | loop fusion | bytes 16777216 | tf_op jit(solution)/shard_map/slice | solution.py:53
  170.4 22.0 %reshape.206 = bf16[4,32,2,8,4,8,64]{6,5,4,3,2,1,0:T(8,128)(2,1)} reshape(bf16[128,2,8,4,512]{4,3,2,1,0:T(4,128)(2,1)} %all-to-all-done) | data formatting | bytes 16777216 | tf_op jit(solution)/shard_map/reshape | solution.py:42
  192.5 8.6 %fusion.1 = bf16[32,4,2,8,64,32,1]{4,5,0,3,2,1,6:T(8,128)(2,1)S(1)} fusion(bf16[4,32,2,8,4,8,64]{6,5,4,3,2,1,0:T(8,128)(2,1)} %reshape.206, bf16[32,4,32,4,8,1,1]{2,4,3,1,0,5,6:T(8,128)(2,1)S(1)} %bitcast.47), kind=kOutput, calls=%fused_computation.4 | convolution fusion | flops 268435456 | bytes 17039360 | tf_op jit(solution)/shard_map/jiasb,sjcqibx->cqjiax/dot_general | solution.py:47
  201.1 8.5 %copy.67 = bf16[32,4,2,8,64,32,1]{4,5,3,2,1,0,6:T(8,128)(2,1)} copy(bf16[32,4,2,8,64,32,1]{4,5,0,3,2,1,6:T(8,128)(2,1)S(1)} %fusion.1) | data formatting | bytes 16777216 | tf_op jit(solution)/shard_map/jiasb,sjcqibx->cqjiax/dot_general | solution.py:47
  209.6 23.4 %reshape.185 = bf16[2,8,128,2048]{3,1,0,2:T(8,128)(2,1)} reshape(bf16[2,8,32,4,32,64]{5,4,1,0,3,2:T(8,128)(2,1)} %bitcast.46) | data formatting | bytes 16777216 | tf_op jit(solution)/shard_map/reshape | solution.py:48
  233.0 15.8 %bitcast_multiply_fusion = f32[2,128,8,2048]{3,1,2,0:T(8,128)S(1)} fusion(bf16[2,8,128,2048]{3,1,0,2:T(8,128)(2,1)} %reshape.185, bf16[1,128,2,128]{3,1,2,0:T(8,128)(2,1)S(1)} %get-tuple-element.10, bf16[1,128,2,128]{3,1,2,0:T(8,128)(2,1)S(1)} %get-tuple-element.9), kind=kOutput, calls=%fused_computation.3 | convolution fusion | flops 2151940096 | bytes 25296896 | tf_op jit(solution)/shard_map/aybr,bqrk->ayqk/dot_general | solution.py:51
  248.8 12.1 %fusion.4 = (bf16[1,128,8,2048]{3,1,2,0:T(8,128)(2,1)}, bf16[1,128,8,2048]{3,1,2,0:T(8,128)(2,1)}) fusion(f32[2,128,8,2048]{3,1,2,0:T(8,128)S(1)} %bitcast_multiply_fusion, bf16[1,128,8,2048]{3,2,1,0:T(8,128)(2,1)} %get-tuple-element.8, bf16[1,128,8,2048]{3,2,1,0:T(8,128)(2,1)} %get-tuple-element.7), kind=kLoop, calls=%fused_computation.12 | loop fusion | flops 20971520 | bytes 33554432 | tf_op jit(solution)/shard_map/convert
  261.0 7.5 %pad_maximum_fusion = bf16[2,128,8,2048]{3,1,2,0:T(8,128)(2,1)} fusion(bf16[1,128,8,2048]{3,1,2,0:T(8,128)(2,1)} %get-tuple-element.6, bf16[1,128,8,2048]{3,1,2,0:T(8,128)(2,1)} %get-tuple-element.5), kind=kLoop, calls=%fused_computation.16 | loop fusion | flops 4194304 | bytes 16777216 | tf_op jit(solution)/shard_map/stack | solution.py:57
  268.4 11.4 %copy.37 = bf16[2,128,8,2048]{3,2,1,0:T(8,128)(2,1)} copy(bf16[2,128,8,2048]{3,1,2,0:T(8,128)(2,1)} %pad_maximum_fusion) | data formatting | bytes 16777216 | tf_op jit(solution)/shard_map/stack | solution.py:57
  (13 shorter events, 0.0 us)
Async XLA Ops:
  0.0 18.2 %copy-start.1 = (bf16[4,1024,512]{2,1,0:T(8,128)(2,1)S(1)}, bf16[4,1024,512]{2,1,0:T(8,128)(2,1)}, u32[]{:S(2)}) copy-start(bf16[4,1024,512]{2,1,0:T(8,128)(2,1)} %param.4) | copy-start | bytes 12582916
  46.1 12.0 %copy-start = (bf16[256,32,32]{0,2,1:T(8,128)(2,1)S(1)}, bf16[256,32,32]{0,2,1:T(8,128)(2,1)}, u32[]{:S(2)}) copy-start(bf16[256,32,32]{0,2,1:T(8,128)(2,1)} %param.6) | copy-start | bytes 1572868
  46.1 15.0 %copy-start.3 = (u32[128]{0:T(128)S(1)}, u32[128]{0:T(128)}, u32[]{:S(2)}) copy-start(u32[128]{0:T(128)} %constant.55) | copy-start | bytes 1540
  46.1 16.3 %copy-start.2 = (s32[4]{0:T(128)S(1)}, s32[4]{0:T(128)}, u32[]{:S(2)}) copy-start(s32[4]{0:T(128)} %param.5) | copy-start | bytes 52
  46.1 124.4 %all-to-all-start = ((bf16[128,2,8,4,512]{4,3,2,1,0:T(4,128)(2,1)}), bf16[128,2,8,4,512]{4,3,2,1,0:T(4,128)(2,1)}, u32[]{:S(2)}, u32[]{:S(2)}) async-start(bf16[128,2,8,4,512]{4,3,2,1,0:T(4,128)(2,1)} %copy.28), calls=%async_computation | async-start | bytes 16777216 | tf_op jit(solution)/shard_map/all_to_all | solution.py:41
